TPU v7x, 32 devices: a whole 2x2x4 slice. The times are simulated.
32 devices in a mesh: prow: 8 (over z, core), pcol: 4 (over y, x).
Axes of the slice: x: 2, y: 2, z: 4, core: 2. Of those that a mesh axis runs over, the one named last changes fastest.
Arguments:
- right_side: float32 [1024, 4, 4, 1024], P('prow', None, 'pcol'), may hold values from -6 to 6
- inverse_blocks: bfloat16 [2, 1, 8, 1024, 2, 4, 1024], P(None, None, 'prow', None, None, 'pcol'), as said below
- coupling: bfloat16 [1, 8, 1024, 2, 4, 1024], P(None, 'prow', None, None, 'pcol'), may hold values from -0.03125 to 0.03125
- pivots: int32 [2, 8, 1024], P(None, 'prow'), may hold values from 0 to 16383, as said below
Outputs:
- solution: bfloat16 [1024, 2, 8, 1024], P('pcol', None, 'prow')
Inputs may be any that keep to these rules, and one draw needn't show every extreme that they name: `inverse_blocks`: each block is unit upper triangular: ones on its diagonal, zeros below it. Every row number of the window appears exactly once; for every p and p2, exactly 16 * 1024 / 8 ** 2 of the entries pivots[:, p, :] are rows g with (g // 1024) % 8 == p2.
All inputs are finite; a program needn't handle non-finite values.
Results may differ from a plain program's by a relative error of at most 0.0052.
Values may be sent and summed in bfloat16 or wider, within the bound.
A program may use at most 128 MiB of HBM per device.

v0:
```python
import jax
import jax.numpy as jnp
from jax import lax
from jax.sharding import PartitionSpec as P


def body(right_side, inverse_blocks, coupling, pivots):
    rhs_here = right_side.shape[0]
    tiles_across = right_side.shape[1]
    tile_width = right_side.shape[3]
    count_rows = inverse_blocks.shape[1] * tile_width
    count_cols = inverse_blocks.shape[4] * tile_width
    blocks_here = inverse_blocks.shape[1]
    inverse_pair = inverse_blocks.reshape(2, count_rows, count_cols)
    coupling_mat = coupling.reshape(count_rows, count_cols)
    flat_rhs = right_side.reshape(rhs_here, tiles_across * tile_width)
    lower_rhs = flat_rhs[:, :count_cols]
    upper_rhs = flat_rhs[:, count_cols:]
    row_devices = lax.axis_size("prow")
    rhs_total = rhs_here * row_devices
    own_cols = rhs_total // lax.axis_size("pcol")
    contract_last = (((1,), (1,)), ((), ()))

    def solve_with(inverse_mat, portion):
        return lax.dot_general(
            portion, inverse_mat, contract_last, preferred_element_type=jnp.float32
        )

    def as_tiles(solved):
        return solved.reshape(own_cols, blocks_here, 1, tile_width)

    first_partial = solve_with(
        inverse_pair[1], lax.all_gather(upper_rhs.astype(jnp.bfloat16), "prow", axis=0, tiled=True)
    )
    upper_solved = lax.psum_scatter(first_partial, "pcol", scatter_dimension=0, tiled=True).astype(
        jnp.bfloat16
    )
    update_partial = jnp.dot(
        lax.all_gather(upper_solved, "pcol", axis=0, tiled=True),
        coupling_mat,
        preferred_element_type=jnp.float32,
    )
    update = lax.psum_scatter(update_partial, "prow", scatter_dimension=0, tiled=True)
    lower_ready = (lower_rhs - update).astype(jnp.bfloat16)
    second_partial = solve_with(
        inverse_pair[0], lax.all_gather(lower_ready, "prow", axis=0, tiled=True)
    )
    lower_solved = lax.psum_scatter(second_partial, "pcol", scatter_dimension=0, tiled=True).astype(
        jnp.bfloat16
    )
    joined = jnp.concatenate([as_tiles(lower_solved), as_tiles(upper_solved)], axis=1)
    all_rows = lax.all_gather(joined, "prow", axis=2, tiled=True).reshape(own_cols, -1)
    permuted = jnp.take(all_rows, pivots.reshape(-1), axis=1)
    return permuted.reshape(own_cols, pivots.shape[0], 1, tile_width)


def solution(mesh):
    in_specs = (
        P("prow", None, "pcol", None),
        P(None, None, "prow", None, None, "pcol", None),
        P(None, "prow", None, None, "pcol", None),
        P(None, "prow", None),
    )
    out_specs = P("pcol", None, "prow", None)
    return jax.shard_map(body, mesh=mesh, in_specs=in_specs, out_specs=out_specs, check_vma=False)
```

profile of v0, /device:TPU:0, one launch (start us, length us, event | category | flops | bytes accessed | tf_op | source)
XLA Modules:
  0.0 492.8 jit_solution(14746014707884761754)
XLA Ops:
  6.5 7.1 %reduce = f32[128,4,1024]{2,1,0:T(4,128)S(1)} reduce(f32[128,4,1,1024]{3,2,1,0:T(1,128)} %param.4, f32[]{:T(128)} %constant.20), dimensions={2}, to_apply=%param.4.reduce_sub_computation | reduce | bytes 4194308 | tf_op args[0]
  13.6 1.6 copy.9
  15.3 1.3 copy-done
  16.6 0.9 slice.27
  17.5 0.2 reduce-scatter.4.cloned.1.call-start
  17.7 7.9 %fusion.1 = (bf16[1,1,1,1024,2,1,1024]{6,4,5,3,2,1,0:T(2,128)(2,1)}, bf16[1,1,1,1024,2,1,1024]{6,4,5,3,2,1,0:T(2,128)(2,1)S(1)}) fusion(bf16[2,1,1,1024,2,1,1024]{6,4,5,3,2,1,0:T(2,128)(2,1)} %param.5), kind=kLoop, calls=%fused_computation.11 | loop fusion | bytes 16777216 | tf_op jit(solution)/shard_map/slice | solution.py:46
  25.7 3.3 copy.10
  29.0 38.2 %all-gather.5.cloned.1.call-done = bf16[1024,2048]{1,0:T(8,128)(2,1)} async-done(((bf16[128,2048]{1,0:T(8,128)(2,1)}), bf16[1024,2048]{1,0:T(8,128)(2,1)}) %all-gather.5.cloned.1.call-update) | async-done | bytes 4194320 | tf_op jit(solution)/shard_map/all_gather | solution.py:33
  67.2 10.0 %fusion.2 = f32[1024,1024]{1,0:T(8,128)} fusion(bf16[1024,2048]{1,0:T(8,128)(2,1)} %all-gather.5.cloned.1.call-done, bf16[1024,2048]{1,0:T(8,128)(2,1)} %bitcast.39), kind=kOutput, calls=%fused_computation.12 | convolution fusion | flops 4294967296 | bytes 12582912 | tf_op jit(solution)/shard_map/dot_general | solution.py:25
  77.2 0.0 all-gather.7.cloned.1.call-start
  77.3 51.5 %reduce-scatter.4.cloned.1.call-done = f32[256,1024]{1,0:T(8,128)} async-done(((f32[1024,1024]{1,0:T(8,128)}), f32[256,1024]{1,0:T(8,128)}) %reduce-scatter.4.cloned.1.call-update) | async-done | bytes 1048592 | tf_op jit(solution)/shard_map/reduce_scatter | solution.py:35
  128.8 2.1 convert_element_type.10
  131.0 5.5 %copy.11 = bf16[128,8,2,1024]{3,1,2,0:T(8,128)(2,1)} copy(bf16[128,8,2,1024]{3,2,1,0:T(2,128)(2,1)} %bitcast.38) | data formatting | bytes 8388608
  136.5 29.7 %all-gather.7.cloned.1.call-done = bf16[1024,1024]{1,0:T(8,128)(2,1)} async-done(((bf16[256,1024]{1,0:T(8,128)(2,1)}), bf16[1024,1024]{1,0:T(8,128)(2,1)}) %all-gather.7.cloned.1.call-update) | async-done | bytes 2097168 | tf_op jit(solution)/shard_map/all_gather | solution.py:39
  166.3 10.5 %fusion.3 = f32[1024,2048]{1,0:T(8,128)} fusion(bf16[1024,1024]{1,0:T(8,128)(2,1)} %all-gather.7.cloned.1.call-done, bf16[1024,2048]{1,0:T(8,128)(2,1)} %bitcast.41), kind=kOutput, calls=%fused_computation.13 | convolution fusion | flops 4294967296 | bytes 14680064 | tf_op jit(solution)/shard_map/dot_general | solution.py:38
  176.9 89.6 %reduce-scatter.6.cloned.1.call-done = f32[128,2048]{1,0:T(8,128)} async-done(((f32[1024,2048]{1,0:T(8,128)}), f32[128,2048]{1,0:T(8,128)}) %reduce-scatter.6.cloned.1.call-update) | async-done | bytes 1048592 | tf_op jit(solution)/shard_map/reduce_scatter | solution.py:43
  266.5 2.1 fusion
  268.7 0.3 reduce-scatter.8.cloned.1.call-start
  268.9 5.5 %copy.12 = bf16[128,8,2,1024]{3,1,2,0:T(8,128)(2,1)} copy(bf16[128,8,2,1024]{3,2,1,0:T(2,128)(2,1)} %bitcast.33) | data formatting | bytes 8388608
  274.5 39.7 %all-gather.9.cloned.1.call-done = bf16[1024,2048]{1,0:T(8,128)(2,1)} async-done(((bf16[128,2048]{1,0:T(8,128)(2,1)}), bf16[1024,2048]{1,0:T(8,128)(2,1)}) %all-gather.9.cloned.1.call-update) | async-done | bytes 4194320 | tf_op jit(solution)/shard_map/all_gather | solution.py:46
  314.1 9.9 %fusion.4 = f32[1024,1024]{1,0:T(8,128)} fusion(bf16[1024,2048]{1,0:T(8,128)(2,1)} %all-gather.9.cloned.1.call-done, bf16[1024,2048]{1,0:T(8,128)(2,1)} %bitcast.40), kind=kOutput, calls=%fused_computation.14 | convolution fusion | flops 4294967296 | bytes 12582912 | tf_op jit(solution)/shard_map/dot_general | solution.py:25
  324.1 0.0 all-gather.11.cloned.1.call-start
  324.2 1.1 copy-done.2
  325.3 0.1 convert_bitcast_fusion.1
  325.4 50.3 %reduce-scatter.8.cloned.1.call-done = f32[256,1024]{1,0:T(8,128)} async-done(((f32[1024,1024]{1,0:T(8,128)}), f32[256,1024]{1,0:T(8,128)}) %reduce-scatter.8.cloned.1.call-update) | async-done | bytes 1048592 | tf_op jit(solution)/shard_map/reduce_scatter | solution.py:48
  375.7 1.3 convert_bitcast_fusion
  377.0 1.1 pad_maximum_fusion
  378.1 82.1 %all-gather.11.cloned.1.call-done = bf16[256,2,8,1024]{3,0,2,1:T(8,128)(2,1)} async-done(((bf16[256,2,1,1024]{3,0,2,1:T(8,128)(2,1)}), bf16[256,2,8,1024]{3,0,2,1:T(8,128)(2,1)}) %all-gather.11.cloned.1.call-update) | async-done | bytes 8388624 | tf_op jit(solution)/shard_map/all_gather | solution.py:52
  460.2 11.6 %copy.6 = bf16[256,2,8,1024]{0,3,2,1:T(8,128)(2,1)} copy(bf16[256,2,8,1024]{3,0,2,1:T(8,128)(2,1)} %all-gather.11.cloned.1.call-done) | data formatting | bytes 16777216 | tf_op jit(solution)/shard_map/all_gather | solution.py:52
  471.8 11.1 %gather_fusion = bf16[2048,256]{1,0:T(8,128)(2,1)S(1)} fusion(bf16[256,16384]{0,1:T(8,128)(2,1)} %bitcast.32, s32[2048]{0:T(1024)S(1)} %broadcast_clamp_fusion), kind=kCustom, calls=%fused_computation | custom fusion | bytes 2105344 | tf_op jit(solution)/shard_map/jit(_take)/gather | solution.py:53
  482.9 1.1 copy.7
  484.1 1.9 broadcast_select_fusion
  (19 shorter events, 0.2 us)
Async XLA Ops:
  6.5 60.7 %all-gather.5.cloned.1.call-start = ((), (), s32[]{:S(2)}) async-start(), calls=%async_computation.3 | async-start | bytes 4718592 | tf_op jit(solution)/shard_map/all_gather | solution.py:33
  15.3 1.3 copy-start
  17.5 111.3 %reduce-scatter.4.cloned.1.call-start = ((), (), s32[]{:S(2)}) async-start(), calls=%async_computation.4 | async-start | bytes 5242880 | tf_op jit(solution)/shard_map/reduce_scatter | solution.py:35
  77.2 89.0 %all-gather.7.cloned.1.call-start = ((), (), s32[]{:S(2)}) async-start(), calls=%async_computation.5 | async-start | bytes 2621440 | tf_op jit(solution)/shard_map/all_gather | solution.py:39
  130.9 135.6 %reduce-scatter.6.cloned.1.call-start = ((), (), s32[]{:S(2)}) async-start(), calls=%async_computation.6 | async-start | bytes 9437184 | tf_op jit(solution)/shard_map/reduce_scatter | solution.py:43
  176.8 89.7 %copy-start.1 = (f32[16,8,4,1024]{3,1,2,0:T(8,128)S(1)}, f32[16,8,4,1024]{3,1,2,0:T(8,128)}, u32[]{:S(2)}) copy-start(f32[16,8,4,1024]{3,1,2,0:T(8,128)} %copy-done) | copy-start | bytes 6291460
  176.8 137.3 %all-gather.9.cloned.1.call-start = ((), (), s32[]{:S(2)}) async-start(), calls=%async_computation.7 | async-start | bytes 4718592 | tf_op jit(solution)/shard_map/all_gather | solution.py:46
  268.7 107.0 %reduce-scatter.8.cloned.1.call-start = ((), (), s32[]{:S(2)}) async-start(), calls=%async_computation.8 | async-start | bytes 5242880 | tf_op jit(solution)/shard_map/reduce_scatter | solution.py:48
  324.1 1.2 copy-start.2
  324.1 53.9 %copy-start.3 = (s32[2,1,1024]{2,1,0:T(1,128)S(1)}, s32[2,1,1024]{2,1,0:T(1,128)}, u32[]{:S(2)}) copy-start(s32[2,1,1024]{2,1,0:T(1,128)} %param.7) | copy-start | bytes 24580
  324.1 136.1 %all-gather.11.cloned.1.call-start = ((), (), s32[]{:S(2)}) async-start(), calls=%async_computation.9 | async-start | bytes 9437184 | tf_op jit(solution)/shard_map/all_gather | solution.py:52
Sparse Core Ops, SparseCore 0:
  17.6 49.5 all-gather.4
  77.4 51.3 reduce-scatter.3
  131.0 35.1 all-gather.6
  176.9 89.5 reduce-scatter.5
  268.8 45.3 all-gather.8
  324.2 51.3 reduce-scatter.7
  378.2 82.0 all-gather.10
where the time goes:
time: 494 us; the launch traced here: 493 us
  waiting for transfers between devices  381 us (77%)
  local copies, waits for them, and re-layouts  51.2 us (10%)
  matrix products  30.4 us (6%)
  other arithmetic  15.6 us (3%)
  between operations  13.6 us (3%)
    reduce_scatter x1, waiting for transfers between devices, body(): lax.psum_scatter(update_partial, 'prow', scatter_dimension=0, tiled=True)  89.6 us
    all_gather x1, waiting for transfers between devices, body(): lax.all_gather(joined, 'prow', axis=2, tiled=True).reshape(own_cols, -1)  82.1 us
    reduce_scatter x1, waiting for transfers between devices, body(): lax.psum_scatter(first_partial, 'pcol', scatter_dimension=0, tiled=True)  51.5 us
    reduce_scatter x1, waiting for transfers between devices, body(): lax.psum_scatter(second_partial, 'pcol', scatter_dimension=0, tiled=True)  50.3 us
    all_gather x1, waiting for transfers between devices, body(): lax.all_gather(lower_ready, 'prow', axis=0, tiled=True)  39.7 us
    all_gather x1, waiting for transfers between devices, body(): lax.all_gather(upper_rhs.astype(jnp.bfloat16), 'prow', axis=0, tiled=True)  38.2 us
    all_gather x1, waiting for transfers between devices, body(): lax.all_gather(upper_solved, 'pcol', axis=0, tiled=True)  29.7 us
    dot_general x2, matrix products, solve_with(): lax.dot_general(portion, inverse_mat, contract_last, preferred_element_ty...  19.9 us
  transfers between devices with their start and end apart: 7, of which 7 were waited for; matrix products, arithmetic and copies ran while one was open for 5% of the time, Pallas kernels for 0%

commit v1 on v0

v1 whole, which is shorter than its diff:
```python
import jax
import jax.numpy as jnp
from jax import lax
from jax.sharding import PartitionSpec as P


def body(right_side, inverse_blocks, coupling, pivots):
    bf16 = jnp.bfloat16
    f32 = jnp.float32
    rhs_here = right_side.shape[0]
    tiles_across = right_side.shape[1]
    tile_width = right_side.shape[3]
    blocks_here = inverse_blocks.shape[1]
    count_rows = blocks_here * tile_width
    tiles_half = inverse_blocks.shape[4]
    count_cols = tiles_half * tile_width
    inverse_pair = inverse_blocks.reshape(2, count_rows, count_cols)
    coupling_mat = coupling.reshape(count_rows, count_cols)
    rows_axis = lax.axis_size("prow")
    cols_axis = lax.axis_size("pcol")
    own_cols = rhs_here * rows_axis // cols_axis
    contract_last = (((1,), (1,)), ((), ()))
    me = lax.axis_index("prow")

    lower_rhs = right_side[:, :tiles_half].reshape(rhs_here, count_cols)
    upper_rhs = right_side[:, tiles_half:].astype(bf16).reshape(rhs_here, count_cols)

    own_pivots = pivots.reshape(-1)
    width = own_pivots.shape[0]
    share = width // rows_axis
    all_pivots = lax.all_gather(own_pivots, "prow", axis=0)

    def owner_of(rows):
        return rows // tile_width % rows_axis

    def local_of(rows):
        return rows // (tile_width * rows_axis) * tile_width + rows % tile_width

    mine = owner_of(all_pivots) == me
    slot = jnp.where(mine, jnp.cumsum(mine.astype(jnp.int32), axis=1) - 1, -1)
    hits = slot[:, :, None] == lax.broadcasted_iota(jnp.int32, (1, 1, share), 2)
    picked = jnp.sum(jnp.where(hits, local_of(all_pivots)[:, :, None], 0), axis=1)
    owner = owner_of(own_pivots)
    same = owner[None, :] == lax.broadcasted_iota(jnp.int32, (rows_axis, 1), 0)
    rank = jnp.sum(jnp.where(same, jnp.cumsum(same.astype(jnp.int32), axis=1) - 1, 0), axis=0)
    code = owner * share + rank

    def solve_with(inverse_mat, portion):
        return lax.dot_general(portion, inverse_mat, contract_last, preferred_element_type=bf16)

    first_partial = solve_with(
        inverse_pair[1], lax.all_gather(upper_rhs, "prow", axis=0, tiled=True)
    )
    upper_solved = lax.psum_scatter(first_partial, "pcol", scatter_dimension=0, tiled=True)
    update_partial = jnp.dot(
        lax.all_gather(upper_solved, "pcol", axis=0, tiled=True),
        coupling_mat,
        preferred_element_type=bf16,
    )
    update = lax.psum_scatter(update_partial, "prow", scatter_dimension=0, tiled=True)
    lower_ready = (lower_rhs - update.astype(f32)).astype(bf16)
    second_partial = solve_with(
        inverse_pair[0], lax.all_gather(lower_ready, "prow", axis=0, tiled=True)
    )
    lower_solved = lax.psum_scatter(second_partial, "pcol", scatter_dimension=0, tiled=True)
    joined = jnp.concatenate([lower_solved, upper_solved], axis=1)
    choose = (
        picked.reshape(-1)[None, :] == lax.broadcasted_iota(jnp.int32, (width, 1), 0)
    ).astype(bf16)
    chosen = jnp.dot(joined, choose, preferred_element_type=bf16)
    received = lax.all_to_all(
        chosen.reshape(own_cols, rows_axis, share), "prow", split_axis=1, concat_axis=1
    ).reshape(own_cols, width)
    place = (
        code[None, :] == lax.broadcasted_iota(jnp.int32, (width, 1), 0)
    ).astype(bf16)
    permuted = jnp.dot(received, place, preferred_element_type=bf16)
    return permuted.reshape(own_cols, pivots.shape[0], 1, tile_width)


def solution(mesh):
    in_specs = (
        P("prow", None, "pcol", None),
        P(None, None, "prow", None, None, "pcol", None),
        P(None, "prow", None, None, "pcol", None),
        P(None, "prow", None),
    )
    out_specs = P("pcol", None, "prow", None)
    return jax.shard_map(body, mesh=mesh, in_specs=in_specs, out_specs=out_specs, check_vma=False)
```

time: 494 us -> 344 us (0.70)
  waiting for transfers between devices: 381 us -> 223 us
  blocking collectives: 0 us -> 14 us
  local copies, waits for them, and re-layouts: 51.2 us -> 37.9 us
  matrix products: 30.4 us -> 36.2 us
    all_gather x2 -> x1, waiting for transfers between devices: 120 us -> 38.3 us  [body(): lax.all_gather(upper_rhs, 'prow', axis=0, tiled=True)]
    reduce_scatter x1, waiting for transfers between devices: 89.6 us -> 45 us  [body(): lax.psum_scatter(update_partial, 'prow', scatter_dimension=0, tiled=True)]
    reduce_scatter x1, waiting for transfers between devices: 50.3 us -> 11.3 us  [body(): lax.psum_scatter(second_partial, 'pcol', scatter_dimension=0, tiled=True)]
    all_to_all x0 -> x1, waiting for transfers between devices: none -> 23.6 us  [body(): lax.all_to_all(chosen.reshape(own_cols, rows_axis, share), 'prow', split_...]
    reduce_scatter x1, waiting for transfers between devices: 51.5 us -> 34.1 us  [body(): lax.psum_scatter(first_partial, 'pcol', scatter_dimension=0, tiled=True)]
    all_gather x0 -> x1, blocking collectives: none -> 14 us  [body(): all_pivots = lax.all_gather(own_pivots, 'prow', axis=0)]
    gather x2 -> x0, local copies, waits for them, and re-layouts: 12.2 us -> none  [body(): permuted = jnp.take(all_rows, pivots.reshape(-1), axis=1)]
    all_gather x1 -> x0, local copies, waits for them, and re-layouts: 11.6 us -> none  [body(): lax.all_gather(joined, 'prow', axis=2, tiled=True).reshape(own_cols, -1)]
  transfers between devices with their start and end apart: 7 -> 7, of which waited for: 7 -> 7; matrix products, arithmetic and copies ran while one was open for 5% -> 11% of each run, Pallas kernels for 0% -> 0%
where the time goes in v1:
time: 344 us; the launch traced here: 343 us
  waiting for transfers between devices  223 us (65%)
  local copies, waits for them, and re-layouts  37.9 us (11%)
  matrix products  36.2 us (11%)
  blocking collectives  14 us (4%)
  between operations  13.6 us (4%)
  other arithmetic  13 us (4%)
  starting transfers between devices  5.24 us (2%)
    reduce_scatter x1, waiting for transfers between devices, body(): lax.psum_scatter(update_partial, 'prow', scatter_dimension=0, tiled=True)  45 us
    all_gather x1, waiting for transfers between devices, body(): lax.all_gather(lower_ready, 'prow', axis=0, tiled=True)  39.6 us
    all_gather x1, waiting for transfers between devices, body(): lax.all_gather(upper_rhs, 'prow', axis=0, tiled=True)  38.3 us
    reduce_scatter x1, waiting for transfers between devices, body(): lax.psum_scatter(first_partial, 'pcol', scatter_dimension=0, tiled=True)  34.1 us
    all_gather x1, waiting for transfers between devices, body(): lax.all_gather(upper_solved, 'pcol', axis=0, tiled=True)  31.2 us
    all_to_all x1, waiting for transfers between devices, body(): lax.all_to_all(chosen.reshape(own_cols, rows_axis, share), 'prow', split_...  23.6 us
    dot_general x2, matrix products, solve_with(): lax.dot_general(portion, inverse_mat, contract_last, preferred_element_ty...  18.7 us
    unnamed x12, local copies, waits for them, and re-layouts  17.4 us
  transfers between devices with their start and end apart: 7, of which 7 were waited for; matrix products, arithmetic and copies ran while one was open for 11% of the time, Pallas kernels for 0%

profile of v1, /device:TPU:0, one launch (start us, length us, event | category | flops | bytes accessed | tf_op | source)
XLA Modules:
  0.0 343.2 jit_solution(7763216155621803395)
XLA Ops:
  6.5 4.5 %fusion.9 = bf16[128,2,1024]{2,1,0:T(2,128)(2,1)S(1)} fusion(f32[128,4,1,1024]{3,2,1,0:T(1,128)} %param.4), kind=kLoop, calls=%fused_computation.12 | loop fusion | bytes 1048576 | tf_op jit(solution)/shard_map/slice | solution.py:26
  11.0 0.9 copy.21
  12.0 8.0 %fusion.32 = (bf16[1,1,1,1024,2,1,1024]{6,4,5,3,2,1,0:T(2,128)(2,1)}, bf16[1,1,1,1024,2,1,1024]{6,4,5,3,2,1,0:T(2,128)(2,1)S(1)}) fusion(bf16[2,1,1,1024,2,1,1024]{6,4,5,3,2,1,0:T(2,128)(2,1)} %param.5), kind=kLoop, calls=%fused_computation.72 | loop fusion | bytes 16777216 | tf_op jit(solution)/shard_map/slice | solution.py:63
  20.0 3.4 copy.22
  23.4 38.3 %all-gather.5.cloned.1.call-done = bf16[1024,2048]{1,0:T(8,128)(2,1)} async-done(((bf16[128,2048]{1,0:T(8,128)(2,1)}), bf16[1024,2048]{1,0:T(8,128)(2,1)}) %all-gather.5.cloned.1.call-update) | async-done | bytes 4194320 | tf_op jit(solution)/shard_map/all_gather | solution.py:52
  61.7 9.4 %fusion.33 = bf16[1024,1024]{1,0:T(8,128)(2,1)} fusion(bf16[1024,2048]{1,0:T(8,128)(2,1)} %all-gather.5.cloned.1.call-done, bf16[1024,2048]{1,0:T(8,128)(2,1)} %bitcast.86), kind=kOutput, calls=%fused_computation.73 | convolution fusion | flops 4294967296 | bytes 10485760 | tf_op jit(solution)/shard_map/dot_general | solution.py:49
  71.2 34.1 %reduce-scatter.4.cloned.1.call-done = bf16[256,1024]{1,0:T(8,128)(2,1)} async-done(((bf16[1024,1024]{1,0:T(8,128)(2,1)}), bf16[256,1024]{1,0:T(8,128)(2,1)}) %reduce-scatter.4.cloned.1.call-update) | async-done | bytes 524304 | tf_op jit(solution)/shard_map/reduce_scatter | solution.py:54
  105.5 5.6 %copy.23 = bf16[128,8,2,1024]{3,1,2,0:T(8,128)(2,1)} copy(bf16[128,8,2,1024]{3,2,1,0:T(2,128)(2,1)} %bitcast.85) | data formatting | bytes 8388608
  111.1 31.2 %all-gather.7.cloned.1.call-done = bf16[1024,1024]{1,0:T(8,128)(2,1)} async-done(((bf16[256,1024]{1,0:T(8,128)(2,1)}), bf16[1024,1024]{1,0:T(8,128)(2,1)}) %all-gather.7.cloned.1.call-update) | async-done | bytes 2097168 | tf_op jit(solution)/shard_map/all_gather | solution.py:56
  142.3 9.3 %fusion.34 = bf16[1024,2048]{1,0:T(8,128)(2,1)} fusion(bf16[1024,1024]{1,0:T(8,128)(2,1)} %all-gather.7.cloned.1.call-done, bf16[1024,2048]{1,0:T(8,128)(2,1)} %bitcast.88), kind=kOutput, calls=%fused_computation.74 | convolution fusion | flops 4294967296 | bytes 10485760 | tf_op jit(solution)/shard_map/dot_general | solution.py:55
  151.7 1.5 copy-done
  153.2 3.2 slice_reduce_fusion
  156.4 0.3 copy.20
  156.8 45.0 %reduce-scatter.6.cloned.1.call-done = bf16[128,2048]{1,0:T(8,128)(2,1)} async-done(((bf16[1024,2048]{1,0:T(8,128)(2,1)}), bf16[128,2048]{1,0:T(8,128)(2,1)}) %reduce-scatter.6.cloned.1.call-update) | async-done | bytes 524304 | tf_op jit(solution)/shard_map/reduce_scatter | solution.py:60
  201.7 1.9 subtract_convert_fusion
  204.0 5.6 %copy.24 = bf16[128,8,2,1024]{3,1,2,0:T(8,128)(2,1)} copy(bf16[128,8,2,1024]{3,2,1,0:T(2,128)(2,1)} %bitcast.83) | data formatting | bytes 8388608
  209.6 39.6 %all-gather.9.cloned.1.call-done = bf16[1024,2048]{1,0:T(8,128)(2,1)} async-done(((bf16[128,2048]{1,0:T(8,128)(2,1)}), bf16[1024,2048]{1,0:T(8,128)(2,1)}) %all-gather.9.cloned.1.call-update) | async-done | bytes 4194320 | tf_op jit(solution)/shard_map/all_gather | solution.py:63
  249.2 9.4 %fusion.35 = bf16[1024,1024]{1,0:T(8,128)(2,1)} fusion(bf16[1024,2048]{1,0:T(8,128)(2,1)} %all-gather.9.cloned.1.call-done, bf16[1024,2048]{1,0:T(8,128)(2,1)} %bitcast.87), kind=kOutput, calls=%fused_computation.75 | convolution fusion | flops 4294967296 | bytes 10485760 | tf_op jit(solution)/shard_map/dot_general | solution.py:49
  258.6 14.0 %all-gather = s32[8,1,2048]{2,1,0:T(1,128)S(1)} all-gather(s32[1,1,2048]{2,1,0:T(1,128)S(1)} %bitcast.94), channel_id=1, replica_groups=mesh['prow'=8,'pcol'=4] {'prow'}, dimensions={0}, use_global_device_ids=true | all-gather | bytes 73728 | tf_op jit(solution)/shard_map/all_gather | solution.py:31
  272.7 2.3 reduce-window.14
  275.0 0.3 slice_reduce_fusion.2
  275.6 5.7 %select_reduce_fusion = s32[8,256]{1,0:T(8,128)S(1)} fusion(s32[8,2048]{1,0:T(8,128)S(1)} %get-tuple-element.9, s32[8,2048]{1,0:T(8,128)S(1)} %get-tuple-element.10), kind=kLoop, calls=%fused_computation.2 | loop fusion | flops 12580864 | bytes 139264 | tf_op jit(solution)/shard_map/reduce_sum | solution.py:42
  281.4 11.3 %reduce-scatter.8.cloned.1.call-done = bf16[256,1024]{1,0:T(8,128)(2,1)} async-done(((bf16[1024,1024]{1,0:T(8,128)(2,1)}), bf16[256,1024]{1,0:T(8,128)(2,1)}) %reduce-scatter.8.cloned.1.call-update) | async-done | bytes 524304 | tf_op jit(solution)/shard_map/reduce_scatter | solution.py:65
  292.7 4.4 %fusion.3 = bf16[256,2048]{1,0:T(8,128)(2,1)S(1)} fusion(s32[2048]{0:T(1024)S(1)} %bitcast.99, bf16[256,1024]{1,0:T(8,128)(2,1)S(1)} %copy-done.1, bf16[256,1024]{1,0:T(8,128)(2,1)} %reduce-scatter.8.cloned.1.call-done), kind=kOutput, calls=%fused_computation.6 | convolution fusion | flops 2153775104 | bytes 2105344 | tf_op jit(solution)/shard_map/dot_general | solution.py:70
  297.1 1.0 copy.38
  298.2 4.6 %all-to-all-start = ((bf16[256,8,256]{2,0,1:T(8,128)(2,1)}), bf16[256,8,256]{2,0,1:T(8,128)(2,1)S(1)}, u32[]{:S(2)}, u32[]{:S(2)}) async-start(bf16[256,8,256]{2,0,1:T(8,128)(2,1)} %bitcast.80), calls=%async_computation.3 | async-start | bytes 2097152 | tf_op jit(solution)/shard_map/all_to_all | solution.py:71
  302.8 2.3 reduce-window.16
  305.7 23.6 %all-to-all-done = bf16[256,8,256]{2,0,1:T(8,128)(2,1)S(1)} async-done(((bf16[256,8,256]{2,0,1:T(8,128)(2,1)}), bf16[256,8,256]{2,0,1:T(8,128)(2,1)S(1)}, u32[]{:S(2)}, u32[]{:S(2)}) %all-to-all-start) | async-done | bytes 1048608 | tf_op jit(solution)/shard_map/all_to_all | solution.py:71
  329.4 0.6 copy.15
  330.0 0.5 reshape.153
  330.5 3.8 %fusion.6 = bf16[256,2,1,1024]{3,0,1,2:T(8,128)(2,1)S(1)} fusion(bf16[256,2048,1]{1,0,2:T(8,128)(2,1)S(1)} %reshape.153, s32[2,1024]{1,0:T(2,128)S(1)} %fusion.27), kind=kOutput, calls=%fused_computation.9 | convolution fusion | flops 2151677952 | bytes 2105344 | tf_op jit(solution)/shard_map/dot_general | solution.py:77
  334.3 2.0 copy.16
  (30 shorter events, 1.8 us)
Async XLA Ops:
  6.5 55.2 %all-gather.5.cloned.1.call-start = ((), (), s32[]{:S(2)}) async-start(), calls=%async_computation.4 | async-start | bytes 4718592 | tf_op jit(solution)/shard_map/all_gather | solution.py:52
  12.0 93.3 %reduce-scatter.4.cloned.1.call-start = ((), (), s32[]{:S(2)}) async-start(), calls=%async_computation.5 | async-start | bytes 2621440 | tf_op jit(solution)/shard_map/reduce_scatter | solution.py:54
  71.1 71.2 %all-gather.7.cloned.1.call-start = ((), (), s32[]{:S(2)}) async-start(), calls=%async_computation.6 | async-start | bytes 2621440 | tf_op jit(solution)/shard_map/all_gather | solution.py:56
  105.3 96.4 %reduce-scatter.6.cloned.1.call-start = ((), (), s32[]{:S(2)}) async-start(), calls=%async_computation.7 | async-start | bytes 4718592 | tf_op jit(solution)/shard_map/reduce_scatter | solution.py:60
  151.6 1.6 copy-start
  151.6 97.5 %all-gather.9.cloned.1.call-start = ((), (), s32[]{:S(2)}) async-start(), calls=%async_computation.8 | async-start | bytes 4718592 | tf_op jit(solution)/shard_map/all_gather | solution.py:63
  203.7 89.0 %reduce-scatter.8.cloned.1.call-start = ((), (), s32[]{:S(2)}) async-start(), calls=%async_computation.9 | async-start | bytes 2621440 | tf_op jit(solution)/shard_map/reduce_scatter | solution.py:65
  249.2 9.4 %copy-start.2 = (s32[2,1,1024]{2,1,0:T(1,128)S(1)}, s32[2,1,1024]{2,1,0:T(1,128)}, u32[]{:S(2)}) copy-start(s32[2,1,1024]{2,1,0:T(1,128)} %param.7) | copy-start | bytes 24580
  249.2 43.5 %copy-start.1 = (bf16[256,1024]{1,0:T(8,128)(2,1)S(1)}, bf16[256,1024]{1,0:T(8,128)(2,1)}, u32[]{:S(2)}) copy-start(bf16[256,1024]{1,0:T(8,128)(2,1)} %reduce-scatter.4.cloned.1.call-done) | copy-start | bytes 1572868
  298.2 31.2 %all-to-all-start = ((bf16[256,8,256]{2,0,1:T(8,128)(2,1)}), bf16[256,8,256]{2,0,1:T(8,128)(2,1)S(1)}, u32[]{:S(2)}, u32[]{:S(2)}) async-start(bf16[256,8,256]{2,0,1:T(8,128)(2,1)} %bitcast.80), calls=%async_computation.3 | async-start | bytes 2097152 | tf_op jit(solution)/shard_map/all_to_all | solution.py:71
Sparse Core Ops, SparseCore 0:
  12.1 49.5 all-gather.4
  71.2 33.9 reduce-scatter.3
  107.1 35.1 all-gather.6
  151.8 49.9 reduce-scatter.5
  203.8 45.3 all-gather.8
  258.7 33.9 reduce-scatter.7

commit v2 on v1

v2 whole, which is shorter than its diff:
```python
import functools

import jax
import jax.numpy as jnp
from jax import lax
from jax.experimental import pallas as pl
from jax.experimental.pallas import tpu as pltpu
from jax.sharding import PartitionSpec as P

BF16 = jnp.bfloat16
F32 = jnp.float32
MESH = pl.DeviceIdType.MESH
PARTS = 2
NT = (((1,), (1,)), ((), ()))
NN = (((1,), (0,)), ((), ()))


def tile_of(size):
    return 256 if size % 256 == 0 else 128


def span(index, size):
    return pl.ds(pl.multiple_of(index * size, size), size)


def meet(sizes):
    barrier = pltpu.get_barrier_semaphore()
    count = 0
    for name, size in sizes:
        place = lax.axis_index(name)
        for step in range(1, size):
            peer = lax.rem(place + step, size)
            pl.semaphore_signal(barrier, inc=1, device_id={name: peer}, device_id_type=MESH)
            count += 1
    pl.semaphore_wait(barrier, count)


def spread_order(size):
    half = size // 2
    return sorted(range(1, size), key=lambda step: (step == half, step))


def start_sums(lhs_ref, mat_ref, own_ref, send_ref, recv_ref, send_sem, recv_sem, size):
    place = lax.axis_index("pcol")
    own, width = own_ref.shape
    tile = tile_of(width)
    part = own // PARTS

    def product(target, store):
        rows = span(target, own)

        @pl.loop(0, width // tile)
        def _(step):
            cols = span(step, tile)
            store(
                cols,
                lax.dot_general(
                    lhs_ref[rows, :], mat_ref[cols, :], NT, preferred_element_type=F32
                ),
            )

    def copy_of(piece, step):
        rows = pl.ds(piece * part, part)
        return pltpu.make_async_remote_copy(
            src_ref=send_ref.at[step - 1, rows],
            dst_ref=recv_ref.at[step - 1, rows],
            send_sem=send_sem.at[piece, step - 1],
            recv_sem=recv_sem.at[piece, step - 1],
            device_id={"pcol": lax.rem(place + step, size)},
            device_id_type=MESH,
        )

    copies = {}
    for step in spread_order(size):

        def keep(cols, value, step=step):
            send_ref[step - 1, :, cols] = value.astype(BF16)

        product(lax.rem(place + step, size), keep)
        copies[0, step] = copy_of(0, step)
        copies[0, step].start()
    for piece in range(1, PARTS):
        for step in spread_order(size):
            copies[piece, step] = copy_of(piece, step)
            copies[piece, step].start()

    def hold(cols, value):
        own_ref[:, cols] = value

    product(place, hold)
    return copies


def finish_sum(copies, piece, own_ref, recv_ref, size):
    own = own_ref.shape[0]
    part = own // PARTS
    rows = pl.ds(piece * part, part)
    for step in spread_order(size):
        copies[piece, step].wait_recv()
    total = own_ref[rows, :]
    for step in range(1, size):
        total = total + recv_ref[step - 1, rows, :].astype(F32)
    return total.astype(BF16)


def upper_kernel(
    size, rhs_ref, inv_ref, coup_ref, upd_ref, solved_ref,
    own_ref, send_ref, recv_ref, full_ref, send_sem, recv_sem, gsend_sem, grecv_sem,
):
    meet((("pcol", size),))
    place = lax.axis_index("pcol")
    own, width = solved_ref.shape
    part = own // PARTS
    count = coup_ref.shape[1]
    tile = tile_of(count)
    copies = start_sums(
        rhs_ref, inv_ref, own_ref, send_ref, recv_ref, send_sem, recv_sem, size
    )
    shares = {}
    for piece in range(PARTS):
        rows = pl.ds(piece * part, part)
        solved_ref[rows, :] = finish_sum(copies, piece, own_ref, recv_ref, size)
        for step in spread_order(size):
            shares[piece, step] = pltpu.make_async_remote_copy(
                src_ref=solved_ref.at[rows],
                dst_ref=full_ref.at[step - 1, rows],
                send_sem=gsend_sem.at[piece, step - 1],
                recv_sem=grecv_sem.at[piece, step - 1],
                device_id={"pcol": lax.rem(place + step, size)},
                device_id_type=MESH,
            )
            shares[piece, step].start()

    def couple(target, block):
        rows = span(target, own)

        @pl.loop(0, count // tile)
        def _(step):
            cols = span(step, tile)
            upd_ref[rows, cols] = lax.dot_general(
                block[...], coup_ref[:, cols], NN, preferred_element_type=F32
            ).astype(BF16)

    couple(place, solved_ref)
    for step in spread_order(size):
        for piece in range(PARTS):
            shares[piece, step].wait_recv()
        couple(lax.rem(place - step + size, size), full_ref.at[step - 1])
    for copy in list(copies.values()) + list(shares.values()):
        copy.wait_send()


def lower_kernel(
    size, line, rhs_ref, inv_ref, upper_ref, picked_ref, code_ref, out_ref,
    own_ref, send_ref, recv_ref, pass_ref, take_ref,
    send_sem, recv_sem, xsend_sem, xrecv_sem,
):
    meet((("pcol", size), ("prow", line)))
    place = lax.axis_index("prow")
    own, width = own_ref.shape
    part = own // PARTS
    share = picked_ref.shape[2]
    count = out_ref.shape[1]
    tile = tile_of(count)
    copies = start_sums(
        rhs_ref, inv_ref, own_ref, send_ref, recv_ref, send_sem, recv_sem, size
    )
    row_ids = lax.broadcasted_iota(jnp.int32, (width, share), 0)
    moves = []
    for piece in range(PARTS):
        rows = pl.ds(piece * part, part)
        lower = finish_sum(copies, piece, own_ref, recv_ref, size)
        upper = upper_ref[rows, :]
        for step in list(range(1, line)) + [0]:
            target = lax.rem(place + step, line)
            wanted = picked_ref[target]
            low = jnp.where(row_ids == wanted, 1.0, 0.0).astype(BF16)
            high = jnp.where(row_ids + width == wanted, 1.0, 0.0).astype(BF16)
            chosen = (
                lax.dot_general(lower, low, NN, preferred_element_type=F32)
                + lax.dot_general(upper, high, NN, preferred_element_type=F32)
            ).astype(BF16)
            if step == 0:
                take_ref[0, rows, :] = chosen
                continue
            pass_ref[step - 1, rows, :] = chosen
            move = pltpu.make_async_remote_copy(
                src_ref=pass_ref.at[step - 1, rows],
                dst_ref=take_ref.at[step, rows],
                send_sem=xsend_sem.at[piece, step - 1],
                recv_sem=xrecv_sem.at[piece, step - 1],
                device_id={"prow": target},
                device_id_type=MESH,
            )
            move.start()
            moves.append(move)
    for move in moves:
        move.wait_recv()
    slot_ids = lax.broadcasted_iota(jnp.int32, (share, tile), 0)

    @pl.loop(0, count // tile)
    def _(step):
        cols = span(step, tile)
        code = code_ref[:, cols]
        total = jnp.zeros((own, tile), F32)
        for source in range(line):
            spot = jnp.where(slot_ids + source * share == code, 1.0, 0.0).astype(BF16)
            total = total + lax.dot_general(
                take_ref[source], spot, NN, preferred_element_type=F32
            )
        out_ref[:, cols] = total.astype(BF16)

    for copy in list(copies.values()) + moves:
        copy.wait_send()


def params(number):
    return pltpu.CompilerParams(
        collective_id=number, has_side_effects=True, vmem_limit_bytes=60 * 1024 * 1024
    )


def in_vmem(count):
    return [pl.BlockSpec(memory_space=pltpu.VMEM)] * count


def sum_scratch(size, own, width):
    return [
        pltpu.VMEM((own, width), F32),
        pltpu.VMEM((size - 1, own, width), BF16),
        pltpu.VMEM((size - 1, own, width), BF16),
    ]


def dma(*shape):
    return pltpu.SemaphoreType.DMA(shape)


def body(right_side, inverse_blocks, coupling, pivots):
    rhs_here = right_side.shape[0]
    tile_width = right_side.shape[3]
    blocks_here = inverse_blocks.shape[1]
    count_rows = blocks_here * tile_width
    tiles_half = inverse_blocks.shape[4]
    count_cols = tiles_half * tile_width
    inverse_pair = inverse_blocks.reshape(2, count_rows, count_cols)
    coupling_mat = coupling.reshape(count_rows, count_cols)
    line = lax.axis_size("prow")
    size = lax.axis_size("pcol")
    rhs_total = rhs_here * line
    own = rhs_total // size
    me = lax.axis_index("prow")

    lower_rhs = right_side[:, :tiles_half].reshape(rhs_here, count_cols)
    upper_rhs = right_side[:, tiles_half:].astype(BF16).reshape(rhs_here, count_cols)

    own_pivots = pivots.reshape(-1)
    width = own_pivots.shape[0]
    share = width // line
    all_pivots = lax.all_gather(own_pivots, "prow", axis=0)

    def owner_of(rows):
        return rows // tile_width % line

    def local_of(rows):
        return rows // (tile_width * line) * tile_width + rows % tile_width

    mine = owner_of(all_pivots) == me
    slot = jnp.where(mine, jnp.cumsum(mine.astype(jnp.int32), axis=1) - 1, -1)
    hits = slot[:, :, None] == lax.broadcasted_iota(jnp.int32, (1, 1, share), 2)
    picked = jnp.sum(jnp.where(hits, local_of(all_pivots)[:, :, None], 0), axis=1)
    owner = owner_of(own_pivots)
    same = owner[None, :] == lax.broadcasted_iota(jnp.int32, (line, 1), 0)
    rank = jnp.sum(jnp.where(same, jnp.cumsum(same.astype(jnp.int32), axis=1) - 1, 0), axis=0)
    code = (me - owner + line) % line * share + rank

    gathered = lax.all_gather(upper_rhs, "prow", axis=0, tiled=True)
    update_partial, upper_solved = pl.pallas_call(
        functools.partial(upper_kernel, size),
        out_shape=(
            jax.ShapeDtypeStruct((rhs_total, count_cols), BF16),
            jax.ShapeDtypeStruct((own, count_rows), BF16),
        ),
        in_specs=in_vmem(3),
        out_specs=tuple(in_vmem(2)),
        scratch_shapes=sum_scratch(size, own, count_rows)
        + [pltpu.VMEM((size - 1, own, count_rows), BF16)]
        + [dma(PARTS, size - 1)] * 4,
        compiler_params=params(0),
        name="upper",
    )(gathered, inverse_pair[1], coupling_mat)
    update = lax.psum_scatter(update_partial, "prow", scatter_dimension=0, tiled=True)
    lower_ready = (lower_rhs - update.astype(F32)).astype(BF16)
    gathered = lax.all_gather(lower_ready, "prow", axis=0, tiled=True)
    permuted = pl.pallas_call(
        functools.partial(lower_kernel, size, line),
        out_shape=jax.ShapeDtypeStruct((own, width), BF16),
        in_specs=in_vmem(5),
        out_specs=in_vmem(1)[0],
        scratch_shapes=sum_scratch(size, own, count_rows)
        + [
            pltpu.VMEM((line - 1, own, share), BF16),
            pltpu.VMEM((line, own, share), BF16),
        ]
        + [dma(PARTS, size - 1)] * 2
        + [dma(PARTS, line - 1)] * 2,
        compiler_params=params(1),
        name="lower",
    )(gathered, inverse_pair[0], upper_solved, picked.reshape(line, 1, share), code.reshape(1, width))
    return permuted.reshape(own, pivots.shape[0], 1, tile_width)


def solution(mesh):
    in_specs = (
        P("prow", None, "pcol", None),
        P(None, None, "prow", None, None, "pcol", None),
        P(None, "prow", None, None, "pcol", None),
        P(None, "prow", None),
    )
    out_specs = P("pcol", None, "prow", None)
    return jax.shard_map(body, mesh=mesh, in_specs=in_specs, out_specs=out_specs, check_vma=False)
```

time: 344 us -> 283 us (0.82)
  waiting for transfers between devices: 223 us -> 91.7 us
  Pallas kernels: 0 us -> 112 us
  matrix products: 36.2 us -> 0 us
  starting transfers between devices: 5.24 us -> 0.27 us
  local copies, waits for them, and re-layouts: 37.9 us -> 34.4 us
    pallas_call x0 -> x2, Pallas kernels: none -> 112 us  [the longest x1 62.8 us: body(): pl.pallas_call(functools.partial(upper_kernel, size), out_shape=(jax.Shap...]
    all_gather x3 -> x2, waiting for transfers between devices: 109 us -> 47.7 us  [the longest x1 35 us: body(): gathered = lax.all_gather(upper_rhs, 'prow', axis=0, tiled=True)]
    reduce_scatter x2 -> x0, waiting for transfers between devices: 45.4 us -> none  [the longest x1 34.1 us: body(): lax.psum_scatter(first_partial, 'pcol', scatter_dimension=0, tiled=True)]
    dot_general x5 -> x0, matrix products: 36.2 us -> none  [the longest x2 18.7 us: solve_with(): lax.dot_general(portion, inverse_mat, contract_last, preferred_element_ty...]
    all_to_all x1 -> x0, waiting for transfers between devices: 23.6 us -> none  [body(): lax.all_to_all(chosen.reshape(own_cols, rows_axis, share), 'prow', split_...]
    all_to_all x1 -> x0, starting transfers between devices: 4.63 us -> none  [body(): lax.all_to_all(chosen.reshape(own_cols, rows_axis, share), 'prow', split_...]
    unnamed x12 -> x11, local copies, waits for them, and re-layouts: 17.4 us -> 15 us
  transfers between devices with their start and end apart: 7 -> 3, of which waited for: 7 -> 3; matrix products, arithmetic and copies ran while one was open for 11% -> 13% of each run, Pallas kernels for 0% -> 0%
where the time goes in v2:
time: 283 us; the launch traced here: 279 us
  Pallas kernels  112 us (40%)
  waiting for transfers between devices  91.7 us (32%)
  local copies, waits for them, and re-layouts  34.4 us (12%)
  blocking collectives  14.2 us (5%)
  other arithmetic  13.6 us (5%)
  between operations  13.2 us (5%)
    pallas_call x1, Pallas kernels, body(): pl.pallas_call(functools.partial(upper_kernel, size), out_shape=(jax.Shap...  62.8 us
    pallas_call x1, Pallas kernels, body(): pl.pallas_call(functools.partial(lower_kernel, size, line), out_shape=jax...  49 us
    reduce_scatter x1, waiting for transfers between devices, body(): lax.psum_scatter(update_partial, 'prow', scatter_dimension=0, tiled=True)  43.9 us
    all_gather x1, waiting for transfers between devices, body(): gathered = lax.all_gather(upper_rhs, 'prow', axis=0, tiled=True)  35 us
    unnamed x11, local copies, waits for them, and re-layouts  15 us
    all_gather x1, blocking collectives, body(): all_pivots = lax.all_gather(own_pivots, 'prow', axis=0)  14.2 us
    all_gather x1, waiting for transfers between devices, body(): gathered = lax.all_gather(lower_ready, 'prow', axis=0, tiled=True)  12.8 us
    slice x1, local copies, waits for them, and re-layouts, body(): inverse_pair[0]  7.96 us
  transfers between devices with their start and end apart: 3, of which 3 were waited for; matrix products, arithmetic and copies ran while one was open for 13% of the time, Pallas kernels for 0%

profile of v2, /device:TPU:0, one launch (start us, length us, event | category | flops | bytes accessed | tf_op | source)
XLA Modules:
  0.0 279.3 jit_solution(13452522500907310704)
XLA Ops:
  6.5 4.5 %fusion = bf16[128,2,1024]{2,1,0:T(2,128)(2,1)S(1)} fusion(f32[128,4,1,1024]{3,2,1,0:T(1,128)} %param.4), kind=kLoop, calls=%fused_computation.3 | loop fusion | bytes 1048576 | tf_op jit(solution)/shard_map/slice | solution.py:255
  11.0 0.9 copy.15
  12.0 0.0 reduce-scatter.2.cloned.1.call-start
  12.0 8.0 %fusion.22 = (bf16[1,1,1,1024,2,1,1024]{6,4,5,3,2,1,0:T(2,128)(2,1)}, bf16[1,1,1,1024,2,1,1024]{6,4,5,3,2,1,0:T(2,128)(2,1)S(1)}) fusion(bf16[2,1,1,1024,2,1,1024]{6,4,5,3,2,1,0:T(2,128)(2,1)} %param.5), kind=kLoop, calls=%fused_computation.64 | loop fusion | bytes 16777216 | tf_op jit(solution)/shard_map/slice | solution.py:309
  20.0 3.4 %copy.16 = bf16[128,8,2,1024]{3,1,2,0:T(8,128)(2,1)} copy(bf16[128,8,2,1024]{3,2,1,0:T(2,128)(2,1)S(1)} %bitcast.60) | data formatting | bytes 8388608
  23.4 3.3 %copy.17 = bf16[128,8,2,1024]{3,1,2,0:T(8,128)(2,1)} copy(bf16[128,8,2,1024]{3,2,1,0:T(2,128)(2,1)S(1)} %bitcast.61) | data formatting | bytes 8388608
  26.8 35.0 %all-gather.4.cloned.1.call-done.rhs_ref = bf16[1024,2048]{1,0:T(8,128)(2,1)} async-done(((bf16[128,2048]{1,0:T(8,128)(2,1)}), bf16[1024,2048]{1,0:T(8,128)(2,1)}) %all-gather.4.cloned.1.call-update) | async-done | bytes 4194320 | tf_op jit(solution)/shard_map/all_gather | solution.py:277
  61.7 62.8 %upper.1 = (bf16[1024,2048]{1,0:T(8,128)(2,1)}, bf16[256,1024]{1,0:T(8,128)(2,1)}) custom-call(bf16[1024,2048]{1,0:T(8,128)(2,1)} %all-gather.4.cloned.1.call-done.rhs_ref, bf16[1024,2048]{1,0:T(8,128)(2,1)} %bitcast.57, bf16[1024,2048]{1,0:T(8,128)(2,1)} %bitcast.58), custom_call_target="tpu_custom_call" | custom-call | tf_op jit(solution)/shard_map/upper/pallas_call | solution.py:278
  124.6 0.2 all-gather.6.cloned.1.call-start
  124.9 1.3 copy-done.1
  126.2 3.2 %slice_reduce_fusion = f32[128,2,1024]{2,1,0:T(2,128)S(1)} fusion(f32[128,4,1,1024]{3,2,1,0:T(1,128)S(1)} %copy-done.1), kind=kLoop, calls=%fused_computation.5 | loop fusion | bytes 2097152 | tf_op jit(solution)/shard_map/slice | solution.py:254
  129.4 0.3 copy.14
  129.8 43.9 %reduce-scatter.2.cloned.1.call-done = bf16[128,2048]{1,0:T(8,128)(2,1)} async-done(((bf16[1024,2048]{1,0:T(8,128)(2,1)}), bf16[128,2048]{1,0:T(8,128)(2,1)}) %reduce-scatter.2.cloned.1.call-update) | async-done | bytes 524304 | tf_op jit(solution)/shard_map/reduce_scatter | solution.py:292
  173.7 1.9 subtract_convert_fusion
  175.7 14.2 %all-gather = s32[8,1,2048]{2,1,0:T(1,128)S(1)} all-gather(s32[1,1,2048]{2,1,0:T(1,128)S(1)} %bitcast.66), channel_id=1, replica_groups=mesh['prow'=8,'pcol'=4] {'prow'}, dimensions={0}, use_global_device_ids=true | all-gather | bytes 73728 | tf_op jit(solution)/shard_map/all_gather | solution.py:260
  189.9 0.1 convert_bitcast_fusion
  190.0 2.3 reduce-window.14
  192.3 0.3 slice_reduce_fusion.2
  192.6 0.2 reduce-window.15
  192.8 0.1 add_bitcast_fusion
  192.9 0.1 fusion.5
  192.9 5.7 %select_reduce_fusion = s32[8,256]{1,0:T(8,128)S(1)} fusion(s32[8,2048]{1,0:T(8,128)S(1)} %get-tuple-element.13, s32[8,2048]{1,0:T(8,128)S(1)} %get-tuple-element.14), kind=kLoop, calls=%fused_computation | loop fusion | flops 12580864 | bytes 139264 | tf_op jit(solution)/shard_map/reduce_sum | solution.py:271
  198.7 0.6 reshape.233.picked_ref
  199.3 2.3 reduce-window.16
  201.6 0.3 slice_reduce_fusion.1
  201.9 0.2 reduce-window.19
  202.1 5.6 %copy.18 = bf16[128,8,2,1024]{3,1,2,0:T(8,128)(2,1)} copy(bf16[128,8,2,1024]{3,2,1,0:T(2,128)(2,1)} %bitcast.59) | data formatting | bytes 8388608
  207.7 0.1 select_reduce_fusion.1
  207.8 0.7 fusion.17.code_ref
  208.5 12.8 %all-gather.6.cloned.1.call-done.rhs_ref = bf16[1024,2048]{1,0:T(8,128)(2,1)} async-done(((bf16[128,2048]{1,0:T(8,128)(2,1)}), bf16[1024,2048]{1,0:T(8,128)(2,1)}) %all-gather.6.cloned.1.call-update) | async-done | bytes 4194320 | tf_op jit(solution)/shard_map/all_gather | solution.py:294
  221.2 49.0 %lower.1 = bf16[256,2048]{1,0:T(8,128)(2,1)} custom-call(bf16[1024,2048]{1,0:T(8,128)(2,1)} %all-gather.6.cloned.1.call-done.rhs_ref, bf16[1024,2048]{1,0:T(8,128)(2,1)} %bitcast.56, bf16[256,1024]{1,0:T(8,128)(2,1)} %get-tuple-element.8.upper_ref, s32[8,1,256]{2,1,0:T(1,128)} %reshape.233.picked_ref, s32[1,2048]{1,0:T(1,128)} %fusion.17.code_ref), custom_call_target="tpu_custom_call" | custom-call | tf_op jit(solution)/shard_map/lower/pallas_call | solution.py:295
  270.2 2.6 reshape.235
  (12 shorter events, 0.1 us)
Async XLA Ops:
  6.5 55.2 %all-gather.4.cloned.1.call-start = ((), (), s32[]{:S(2)}) async-start(), calls=%async_computation.1 | async-start | bytes 4718592 | tf_op jit(solution)/shard_map/all_gather | solution.py:277
  12.0 161.7 %reduce-scatter.2.cloned.1.call-start = ((), (), s32[]{:S(2)}) async-start(), calls=%async_computation.2 | async-start | bytes 4718592 | tf_op jit(solution)/shard_map/reduce_scatter | solution.py:292
  20.0 3.4 %copy-start = (bf16[1,1,1024,2,1,1024]{5,3,4,2,1,0:T(2,128)(2,1)S(1)}, bf16[1,1,1024,2,1,1024]{5,3,4,2,1,0:T(2,128)(2,1)}, u32[]{:S(2)}) copy-start(bf16[1,1,1024,2,1,1024]{5,3,4,2,1,0:T(2,128)(2,1)} %param.6) | copy-start | bytes 12582916
  124.6 1.6 copy-start.1
  124.6 51.0 %copy-start.2 = (s32[2,1,1024]{2,1,0:T(1,128)S(1)}, s32[2,1,1024]{2,1,0:T(1,128)}, u32[]{:S(2)}) copy-start(s32[2,1,1024]{2,1,0:T(1,128)} %param.7) | copy-start | bytes 24580
  124.6 96.6 %all-gather.6.cloned.1.call-start = ((), (), s32[]{:S(2)}) async-start(), calls=%async_computation.3 | async-start | bytes 4718592 | tf_op jit(solution)/shard_map/all_gather | solution.py:294
Sparse Core Ops, SparseCore 0:
  12.1 49.5 all-gather.3
  124.8 48.8 reduce-scatter.1
  175.8 45.4 all-gather.5

commit v3 on v2

--- a/solution.py
+++ b/solution.py
@@ -11,6 +11,7 @@
 F32 = jnp.float32
 MESH = pl.DeviceIdType.MESH
 PARTS = 2
+CORES = 2
 NT = (((1,), (1,)), ((), ()))
 NN = (((1,), (0,)), ((), ()))
 
@@ -104,50 +105,122 @@
 
 
 def upper_kernel(
-    size, rhs_ref, inv_ref, coup_ref, upd_ref, solved_ref,
-    own_ref, send_ref, recv_ref, full_ref, send_sem, recv_sem, gsend_sem, grecv_sem,
+    size, line, rhs_ref, inv_ref, coup_ref, upd_ref, solved_ref,
+    all_ref, prod_ref, own_ref, send_ref, recv_ref, full_ref,
+    rsend_sem, rrecv_sem, psend_sem, precv_sem, send_sem, recv_sem, gsend_sem, grecv_sem,
 ):
-    meet((("pcol", size),))
+    chips = line // CORES
+    here = lax.axis_index("prow")
     place = lax.axis_index("pcol")
-    own, width = solved_ref.shape
-    part = own // PARTS
+    chip = here // CORES
+    core = lax.rem(here, CORES)
+    right = lax.rem(chip + 1, chips) * CORES + core
+    left = lax.rem(chip + chips - 1, chips) * CORES + core
+    partner = chip * CORES + (CORES - 1 - core)
+    peers = [lax.rem(place + step, size) for step in range(1, size)]
+
+    barrier = pltpu.get_barrier_semaphore()
+    for device in (right, left, partner):
+        pl.semaphore_signal(barrier, inc=1, device_id={"prow": device}, device_id_type=MESH)
+    for device in peers:
+        pl.semaphore_signal(barrier, inc=1, device_id={"pcol": device}, device_id_type=MESH)
+    pl.semaphore_wait(barrier, 3 + len(peers))
+
+    rhs_here, depth = rhs_ref.shape
+    rows = CORES * rhs_here
+    part = rows // size
+    width = inv_ref.shape[0]
     count = coup_ref.shape[1]
-    tile = tile_of(count)
-    copies = start_sums(
-        rhs_ref, inv_ref, own_ref, send_ref, recv_ref, send_sem, recv_sem, size
-    )
-    shares = {}
-    for piece in range(PARTS):
-        rows = pl.ds(piece * part, part)
-        solved_ref[rows, :] = finish_sum(copies, piece, own_ref, recv_ref, size)
-        for step in spread_order(size):
-            shares[piece, step] = pltpu.make_async_remote_copy(
-                src_ref=solved_ref.at[rows],
-                dst_ref=full_ref.at[step - 1, rows],
-                send_sem=gsend_sem.at[piece, step - 1],
-                recv_sem=grecv_sem.at[piece, step - 1],
-                device_id={"pcol": lax.rem(place + step, size)},
-                device_id_type=MESH,
-            )
-            shares[piece, step].start()
-
-    def couple(target, block):
-        rows = span(target, own)
-
-        @pl.loop(0, count // tile)
+    tile = tile_of(width)
+    wide = tile_of(count)
+
+    def remote(src, dst, sends, recvs, axis, device):
+        return pltpu.make_async_remote_copy(
+            src_ref=src, dst_ref=dst, send_sem=sends, recv_sem=recvs,
+            device_id={axis: device}, device_id_type=MESH,
+        )
+
+    ring, pairs, sums, shares = {}, {}, {}, {}
+
+    def chip_of(stage):
+        return lax.rem(chip + chips - stage, chips)
+
+    def collect(stage):
+        slot = chip_of(stage) * CORES + core
+        source = rhs_ref if stage == 0 else all_ref.at[slot]
+        if stage > 0:
+            ring[stage - 1].wait_recv()
+        if stage < chips - 1:
+            ring[stage] = remote(
+                source, all_ref.at[slot], rsend_sem.at[stage], rrecv_sem.at[stage], "prow", right
+            )
+            ring[stage].start()
+        pairs[stage] = remote(
+            source, all_ref.at[slot], psend_sem.at[stage], precv_sem.at[stage], "prow", partner
+        )
+        pairs[stage].start()
+        if stage == 0:
+            all_ref[slot] = rhs_ref[...]
+        pairs[stage].wait_recv()
+
+    def multiply(stage):
+        first = chip_of(stage) * CORES
+
+        @pl.loop(0, width // tile)
         def _(step):
             cols = span(step, tile)
-            upd_ref[rows, cols] = lax.dot_general(
-                block[...], coup_ref[:, cols], NN, preferred_element_type=F32
+            lhs = all_ref[pl.ds(first, CORES)].reshape(rows, depth)
+            value = lax.dot_general(lhs, inv_ref[cols, :], NT, preferred_element_type=F32)
+            for owner in range(size):
+                piece = value[owner * part : (owner + 1) * part]
+                prod_ref[owner, :, cols] = piece
+                send_ref[stage, owner, :, cols] = piece.astype(BF16)
+
+        own_ref[stage] = prod_ref[place]
+        for index, peer in enumerate(peers):
+            sums[stage, index] = remote(
+                send_ref.at[stage, peer], recv_ref.at[stage, index],
+                send_sem.at[stage, index], recv_sem.at[stage, index], "pcol", peer,
+            )
+            sums[stage, index].start()
+
+    def settle(stage):
+        total = own_ref[stage]
+        for index in range(size - 1):
+            sums[stage, index].wait_recv()
+            total = total + recv_ref[stage, index].astype(F32)
+        full_ref[stage, place] = total.astype(BF16)
+        for index, peer in enumerate(peers):
+            shares[stage, index] = remote(
+                full_ref.at[stage, place], full_ref.at[stage, place],
+                gsend_sem.at[stage, index], grecv_sem.at[stage, index], "pcol", peer,
+            )
+            shares[stage, index].start()
+
+    def couple(stage):
+        for index in range(size - 1):
+            shares[stage, index].wait_recv()
+        target = span(chip_of(stage), rows)
+        solved_ref[target, :] = full_ref[stage].reshape(rows, width)
+
+        @pl.loop(0, count // wide)
+        def _(step):
+            cols = span(step, wide)
+            upd_ref[target, cols] = lax.dot_general(
+                solved_ref[target, :], coup_ref[:, cols], NN, preferred_element_type=F32
             ).astype(BF16)
 
-    couple(place, solved_ref)
-    for step in spread_order(size):
-        for piece in range(PARTS):
-            shares[piece, step].wait_recv()
-        couple(lax.rem(place - step + size, size), full_ref.at[step - 1])
-    for copy in list(copies.values()) + list(shares.values()):
-        copy.wait_send()
+    for stage in range(chips + 2):
+        if stage < chips:
+            collect(stage)
+            multiply(stage)
+        if 1 <= stage <= chips:
+            settle(stage - 1)
+        if stage >= 2:
+            couple(stage - 2)
+    for group in (ring, pairs, sums, shares):
+        for copy in group.values():
+            copy.wait_send()
 
 
 def lower_kernel(
@@ -274,21 +347,31 @@
     rank = jnp.sum(jnp.where(same, jnp.cumsum(same.astype(jnp.int32), axis=1) - 1, 0), axis=0)
     code = (me - owner + line) % line * share + rank
 
-    gathered = lax.all_gather(upper_rhs, "prow", axis=0, tiled=True)
-    update_partial, upper_solved = pl.pallas_call(
-        functools.partial(upper_kernel, size),
+    chips = line // CORES
+    part = CORES * rhs_here // size
+    update_partial, upper_all = pl.pallas_call(
+        functools.partial(upper_kernel, size, line),
         out_shape=(
             jax.ShapeDtypeStruct((rhs_total, count_cols), BF16),
-            jax.ShapeDtypeStruct((own, count_rows), BF16),
+            jax.ShapeDtypeStruct((rhs_total, count_rows), BF16),
         ),
         in_specs=in_vmem(3),
         out_specs=tuple(in_vmem(2)),
-        scratch_shapes=sum_scratch(size, own, count_rows)
-        + [pltpu.VMEM((size - 1, own, count_rows), BF16)]
-        + [dma(PARTS, size - 1)] * 4,
+        scratch_shapes=[
+            pltpu.VMEM((line, rhs_here, count_cols), BF16),
+            pltpu.VMEM((size, part, count_rows), F32),
+            pltpu.VMEM((chips, part, count_rows), F32),
+            pltpu.VMEM((chips, size, part, count_rows), BF16),
+            pltpu.VMEM((chips, size - 1, part, count_rows), BF16),
+            pltpu.VMEM((chips, size, part, count_rows), BF16),
+        ]
+        + [dma(chips - 1)] * 2
+        + [dma(chips)] * 2
+        + [dma(chips, size - 1)] * 4,
         compiler_params=params(0),
         name="upper",
-    )(gathered, inverse_pair[1], coupling_mat)
+    )(upper_rhs, inverse_pair[1], coupling_mat)
+    upper_solved = lax.dynamic_slice_in_dim(upper_all, lax.axis_index("pcol") * own, own, 0)
     update = lax.psum_scatter(update_partial, "prow", scatter_dimension=0, tiled=True)
     lower_ready = (lower_rhs - update.astype(F32)).astype(BF16)
     gathered = lax.all_gather(lower_ready, "prow", axis=0, tiled=True)

time: 283 us -> 257 us (0.908)
  waiting for transfers between devices: 91.7 us -> 56.8 us
  Pallas kernels: 112 us -> 121 us
    all_gather x1 -> x0, waiting for transfers between devices: 35 us -> none  [body(): gathered = lax.all_gather(upper_rhs, 'prow', axis=0, tiled=True)]
    pallas_call x1, Pallas kernels: 62.8 us -> 71.9 us  [body(): pl.pallas_call(functools.partial(upper_kernel, size, line), out_shape=(ja...]
  transfers between devices with their start and end apart: 3 -> 2, of which waited for: 3 -> 2; matrix products, arithmetic and copies ran while one was open for 13% -> 9% of each run, Pallas kernels for 0% -> 0%
where the time goes in v3:
time: 257 us; the launch traced here: 253 us
  Pallas kernels  121 us (47%)
  waiting for transfers between devices  56.8 us (22%)
  local copies, waits for them, and re-layouts  33.9 us (13%)
  blocking collectives  14.2 us (6%)
  other arithmetic  13.6 us (5%)
  between operations  13.5 us (5%)
    pallas_call x1, Pallas kernels, body(): pl.pallas_call(functools.partial(upper_kernel, size, line), out_shape=(ja...  71.9 us
    pallas_call x1, Pallas kernels, body(): pl.pallas_call(functools.partial(lower_kernel, size, line), out_shape=jax...  49 us
    reduce_scatter x1, waiting for transfers between devices, body(): lax.psum_scatter(update_partial, 'prow', scatter_dimension=0, tiled=True)  45.9 us
    all_gather x1, blocking collectives, body(): all_pivots = lax.all_gather(own_pivots, 'prow', axis=0)  14.2 us
    unnamed x11, local copies, waits for them, and re-layouts  13.7 us
    all_gather x1, waiting for transfers between devices, body(): gathered = lax.all_gather(lower_ready, 'prow', axis=0, tiled=True)  10.9 us
    slice x1, local copies, waits for them, and re-layouts, body(): inverse_pair[0]  7.95 us
    reduce_sum x1, other arithmetic, body(): jnp.sum(jnp.where(hits, local_of(all_pivots)[:, :, None], 0), axis=1)  5.74 us
  transfers between devices with their start and end apart: 2, of which 2 were waited for; matrix products, arithmetic and copies ran while one was open for 9% of the time, Pallas kernels for 0%

profile of v3, /device:TPU:0, one launch (start us, length us, event | category | flops | bytes accessed | tf_op | source)
XLA Modules:
  0.0 253.2 jit_solution(17135909872828901210)
XLA Ops:
  6.5 7.9 %fusion.22 = (bf16[1,1,1,1024,2,1,1024]{6,4,5,3,2,1,0:T(2,128)(2,1)}, bf16[1,1,1,1024,2,1,1024]{6,4,5,3,2,1,0:T(2,128)(2,1)S(1)}) fusion(bf16[2,1,1,1024,2,1,1024]{6,4,5,3,2,1,0:T(2,128)(2,1)} %param.5), kind=kLoop, calls=%fused_computation.65 | loop fusion | bytes 16777216 | tf_op jit(solution)/shard_map/slice | solution.py:392
  14.5 3.4 %copy.16 = bf16[128,8,2,1024]{3,1,2,0:T(8,128)(2,1)} copy(bf16[128,8,2,1024]{3,2,1,0:T(2,128)(2,1)S(1)} %bitcast.60) | data formatting | bytes 8388608
  17.9 3.4 %copy.17 = bf16[128,8,2,1024]{3,1,2,0:T(8,128)(2,1)} copy(bf16[128,8,2,1024]{3,2,1,0:T(2,128)(2,1)S(1)} %bitcast.61) | data formatting | bytes 8388608
  21.4 3.2 %fusion = bf16[128,2,1024]{2,1,0:T(2,128)(2,1)S(1)} fusion(f32[128,4,1,1024]{3,2,1,0:T(1,128)S(1)} %copy-done.1), kind=kLoop, calls=%fused_computation.3 | loop fusion | bytes 1048576 | tf_op jit(solution)/shard_map/slice | solution.py:328
  24.6 0.9 copy.15
  25.5 71.9 %upper.1 = (bf16[1024,2048]{1,0:T(8,128)(2,1)}, bf16[1024,1024]{1,0:T(8,128)(2,1)}) custom-call(bf16[128,2048]{1,0:T(8,128)(2,1)} %bitcast.64, bf16[1024,2048]{1,0:T(8,128)(2,1)} %bitcast.57, bf16[1024,2048]{1,0:T(8,128)(2,1)} %bitcast.58), custom_call_target="tpu_custom_call" | custom-call | tf_op jit(solution)/shard_map/upper/pallas_call | solution.py:352
  97.4 0.0 reduce-scatter.2.cloned.1.call-update
  97.5 0.2 all-gather.3.cloned.1.call-start
  97.7 3.2 %slice_reduce_fusion = f32[128,2,1024]{2,1,0:T(2,128)S(1)} fusion(f32[128,4,1,1024]{3,2,1,0:T(1,128)S(1)} %copy-done.1), kind=kLoop, calls=%fused_computation.5 | loop fusion | bytes 2097152 | tf_op jit(solution)/shard_map/slice | solution.py:327
  100.9 0.3 copy.14
  101.3 45.9 %reduce-scatter.2.cloned.1.call-done = bf16[128,2048]{1,0:T(8,128)(2,1)} async-done(((bf16[1024,2048]{1,0:T(8,128)(2,1)}), bf16[128,2048]{1,0:T(8,128)(2,1)}) %reduce-scatter.2.cloned.1.call-update) | async-done | bytes 524304 | tf_op jit(solution)/shard_map/reduce_scatter | solution.py:375
  147.2 1.9 subtract_convert_fusion
  149.1 0.0 all-gather.3.cloned.1.call-update
  149.2 14.2 %all-gather = s32[8,1,2048]{2,1,0:T(1,128)S(1)} all-gather(s32[1,1,2048]{2,1,0:T(1,128)S(1)} %bitcast.66), channel_id=1, replica_groups=mesh['prow'=8,'pcol'=4] {'prow'}, dimensions={0}, use_global_device_ids=true | all-gather | bytes 73728 | tf_op jit(solution)/shard_map/all_gather | solution.py:333
  163.4 0.1 convert_bitcast_fusion
  163.5 2.3 reduce-window.14
  165.8 0.3 slice_reduce_fusion.2
  166.1 0.2 reduce-window.15
  166.3 0.1 add_bitcast_fusion
  166.4 0.1 fusion.5
  166.5 5.7 %select_reduce_fusion = s32[8,256]{1,0:T(8,128)S(1)} fusion(s32[8,2048]{1,0:T(8,128)S(1)} %get-tuple-element.13, s32[8,2048]{1,0:T(8,128)S(1)} %get-tuple-element.14), kind=kLoop, calls=%fused_computation | loop fusion | flops 12580864 | bytes 139264 | tf_op jit(solution)/shard_map/reduce_sum | solution.py:344
  172.2 0.6 reshape.233.picked_ref
  172.8 2.3 reduce-window.16
  175.1 0.3 slice_reduce_fusion.1
  175.4 0.2 reduce-window.19
  175.6 5.6 %copy.18 = bf16[128,8,2,1024]{3,1,2,0:T(8,128)(2,1)} copy(bf16[128,8,2,1024]{3,2,1,0:T(2,128)(2,1)} %bitcast.59) | data formatting | bytes 8388608
  181.2 0.1 select_reduce_fusion.1
  181.3 1.9 constant_dynamic-slice_fusion.upper_ref
  183.2 0.7 fusion.17.code_ref
  183.9 10.9 %all-gather.3.cloned.1.call-done.rhs_ref = bf16[1024,2048]{1,0:T(8,128)(2,1)} async-done(((bf16[128,2048]{1,0:T(8,128)(2,1)}), bf16[1024,2048]{1,0:T(8,128)(2,1)}) %all-gather.3.cloned.1.call-update) | async-done | bytes 4194320 | tf_op jit(solution)/shard_map/all_gather | solution.py:377
  194.7 49.0 %lower.1 = bf16[256,2048]{1,0:T(8,128)(2,1)} custom-call(bf16[1024,2048]{1,0:T(8,128)(2,1)} %all-gather.3.cloned.1.call-done.rhs_ref, bf16[1024,2048]{1,0:T(8,128)(2,1)} %bitcast.56, bf16[256,1024]{1,0:T(8,128)(2,1)} %constant_dynamic-slice_fusion.upper_ref, s32[8,1,256]{2,1,0:T(1,128)} %reshape.233.picked_ref, s32[1,2048]{1,0:T(1,128)} %fusion.17.code_ref), custom_call_target="tpu_custom_call" | custom-call | tf_op jit(solution)/shard_map/lower/pallas_call | solution.py:378
  243.7 2.6 %reshape.235 = bf16[256,2,1,1024]{3,1,0,2:T(2,128)(2,1)} reshape(bf16[256,2048]{1,0:T(8,128)(2,1)} %lower.1) | data formatting | bytes 2097152 | tf_op jit(solution)/shard_map/reshape | solution.py:393
  (10 shorter events, 0.1 us)
Async XLA Ops:
  6.5 140.7 %reduce-scatter.2.cloned.1.call-start = ((), (), s32[]{:S(2)}) async-start(), calls=%async_computation.1 | async-start | bytes 4718592 | tf_op jit(solution)/shard_map/reduce_scatter | solution.py:375
  14.5 3.5 %copy-start = (bf16[1,1,1024,2,1,1024]{5,3,4,2,1,0:T(2,128)(2,1)S(1)}, bf16[1,1,1024,2,1,1024]{5,3,4,2,1,0:T(2,128)(2,1)}, u32[]{:S(2)}) copy-start(bf16[1,1,1024,2,1,1024]{5,3,4,2,1,0:T(2,128)(2,1)} %param.6) | copy-start | bytes 12582916
  17.9 3.4 %copy-start.1 = (f32[128,4,1,1024]{3,2,1,0:T(1,128)S(1)}, f32[128,4,1,1024]{3,2,1,0:T(1,128)}, u32[]{:S(2)}) copy-start(f32[128,4,1,1024]{3,2,1,0:T(1,128)} %param.4) | copy-start | bytes 6291460
  97.5 51.7 %copy-start.2 = (s32[2,1,1024]{2,1,0:T(1,128)S(1)}, s32[2,1,1024]{2,1,0:T(1,128)}, u32[]{:S(2)}) copy-start(s32[2,1,1024]{2,1,0:T(1,128)} %param.7) | copy-start | bytes 24580
  97.5 97.2 %all-gather.3.cloned.1.call-start = ((), (), s32[]{:S(2)}) async-start(), calls=%async_computation.2 | async-start | bytes 4718592 | tf_op jit(solution)/shard_map/all_gather | solution.py:377
Sparse Core Ops, SparseCore 0:
  97.6 49.5 reduce-scatter.1
  149.3 45.4 all-gather.2

commit v4 on v3

--- a/solution.py
+++ b/solution.py
@@ -46,9 +46,10 @@
     own, width = own_ref.shape
     tile = tile_of(width)
     part = own // PARTS
+    each = own // lhs_ref.shape[1]
 
     def product(target, store):
-        rows = span(target, own)
+        sources = pl.ds(target * each, each)
 
         @pl.loop(0, width // tile)
         def _(step):
@@ -56,7 +57,10 @@
             store(
                 cols,
                 lax.dot_general(
-                    lhs_ref[rows, :], mat_ref[cols, :], NT, preferred_element_type=F32
+                    lhs_ref[sources].reshape(own, lhs_ref.shape[2]),
+                    mat_ref[cols, :],
+                    NT,
+                    preferred_element_type=F32,
                 ),
             )
 
@@ -225,8 +229,8 @@
 
 def lower_kernel(
     size, line, rhs_ref, inv_ref, upper_ref, picked_ref, code_ref, out_ref,
-    own_ref, send_ref, recv_ref, pass_ref, take_ref,
-    send_sem, recv_sem, xsend_sem, xrecv_sem,
+    own_ref, send_ref, recv_ref, pass_ref, take_ref, all_ref,
+    rsend_sem, rrecv_sem, psend_sem, precv_sem, send_sem, recv_sem, xsend_sem, xrecv_sem,
 ):
     meet((("pcol", size), ("prow", line)))
     place = lax.axis_index("prow")
@@ -235,8 +239,40 @@
     share = picked_ref.shape[2]
     count = out_ref.shape[1]
     tile = tile_of(count)
+    chips = line // CORES
+    chip = place // CORES
+    core = lax.rem(place, CORES)
+    right = lax.rem(chip + 1, chips) * CORES + core
+    partner = chip * CORES + (CORES - 1 - core)
+    ring, pairs = [], []
+    for stage in range(chips):
+        slot = lax.rem(chip + chips - stage, chips) * CORES + core
+        source = rhs_ref if stage == 0 else all_ref.at[slot]
+        if stage > 0:
+            ring[stage - 1].wait_recv()
+        if stage < chips - 1:
+            ring.append(
+                pltpu.make_async_remote_copy(
+                    src_ref=source, dst_ref=all_ref.at[slot],
+                    send_sem=rsend_sem.at[stage], recv_sem=rrecv_sem.at[stage],
+                    device_id={"prow": right}, device_id_type=MESH,
+                )
+            )
+            ring[stage].start()
+        pairs.append(
+            pltpu.make_async_remote_copy(
+                src_ref=source, dst_ref=all_ref.at[slot],
+                send_sem=psend_sem.at[stage], recv_sem=precv_sem.at[stage],
+                device_id={"prow": partner}, device_id_type=MESH,
+            )
+        )
+        pairs[stage].start()
+        if stage == 0:
+            all_ref[slot] = rhs_ref[...]
+    for copy in pairs:
+        copy.wait_recv()
     copies = start_sums(
-        rhs_ref, inv_ref, own_ref, send_ref, recv_ref, send_sem, recv_sem, size
+        all_ref, inv_ref, own_ref, send_ref, recv_ref, send_sem, recv_sem, size
     )
     row_ids = lax.broadcasted_iota(jnp.int32, (width, share), 0)
     moves = []
@@ -283,7 +319,7 @@
             )
         out_ref[:, cols] = total.astype(BF16)
 
-    for copy in list(copies.values()) + moves:
+    for copy in ring + pairs + list(copies.values()) + moves:
         copy.wait_send()
 
 
@@ -374,7 +410,8 @@
     upper_solved = lax.dynamic_slice_in_dim(upper_all, lax.axis_index("pcol") * own, own, 0)
     update = lax.psum_scatter(update_partial, "prow", scatter_dimension=0, tiled=True)
     lower_ready = (lower_rhs - update.astype(F32)).astype(BF16)
-    gathered = lax.all_gather(lower_ready, "prow", axis=0, tiled=True)
+    later_pair, _ = lax.optimization_barrier((inverse_blocks, update_partial))
+    later_inverse = later_pair[0].reshape(count_rows, count_cols)
     permuted = pl.pallas_call(
         functools.partial(lower_kernel, size, line),
         out_shape=jax.ShapeDtypeStruct((own, width), BF16),
@@ -384,12 +421,15 @@
         + [
             pltpu.VMEM((line - 1, own, share), BF16),
             pltpu.VMEM((line, own, share), BF16),
+            pltpu.VMEM((line, rhs_here, count_cols), BF16),
         ]
+        + [dma(chips - 1)] * 2
+        + [dma(chips)] * 2
         + [dma(PARTS, size - 1)] * 2
         + [dma(PARTS, line - 1)] * 2,
         compiler_params=params(1),
         name="lower",
-    )(gathered, inverse_pair[0], upper_solved, picked.reshape(line, 1, share), code.reshape(1, width))
+    )(lower_ready, later_inverse, upper_solved, picked.reshape(line, 1, share), code.reshape(1, width))
     return permuted.reshape(own, pivots.shape[0], 1, tile_width)
 
 

time: 257 us -> 244 us (0.949)
  waiting for transfers between devices: 56.8 us -> 10.9 us
  Pallas kernels: 121 us -> 158 us
  local copies, waits for them, and re-layouts: 33.9 us -> 28.8 us
    pallas_call x1, Pallas kernels: 49 us -> 85.7 us  [body(): pl.pallas_call(functools.partial(lower_kernel, size, line), out_shape=jax...]
    reduce_scatter x1, waiting for transfers between devices: 45.9 us -> 10.9 us  [body(): lax.psum_scatter(update_partial, 'prow', scatter_dimension=0, tiled=True)]
    all_gather x1 -> x0, waiting for transfers between devices: 10.9 us -> none  [body(): gathered = lax.all_gather(lower_ready, 'prow', axis=0, tiled=True)]
    slice x2 -> x5, local copies, waits for them, and re-layouts: 8.24 us -> 4.72 us  [the longest x2 2.25 us: body(): later_inverse = later_pair[0].reshape(count_rows, count_cols)]
  transfers between devices with their start and end apart: 2 -> 1, of which waited for: 2 -> 1; matrix products, arithmetic and copies ran while one was open for 9% -> 9% of each run, Pallas kernels for 0% -> 0%
where the time goes in v4:
time: 244 us; the launch traced here: 239 us
  Pallas kernels  158 us (65%)
  local copies, waits for them, and re-layouts  28.8 us (12%)
  blocking collectives  14.5 us (6%)
  other arithmetic  13.6 us (6%)
  between operations  13.5 us (6%)
  waiting for transfers between devices  10.9 us (4%)
    pallas_call x1, Pallas kernels, body(): pl.pallas_call(functools.partial(lower_kernel, size, line), out_shape=jax...  85.7 us
    pallas_call x1, Pallas kernels, body(): pl.pallas_call(functools.partial(upper_kernel, size, line), out_shape=(ja...  71.9 us
    all_gather x1, blocking collectives, body(): all_pivots = lax.all_gather(own_pivots, 'prow', axis=0)  14.5 us
    unnamed x11, local copies, waits for them, and re-layouts  12.2 us
    reduce_scatter x1, waiting for transfers between devices, body(): lax.psum_scatter(update_partial, 'prow', scatter_dimension=0, tiled=True)  10.9 us
    reduce_sum x1, other arithmetic, body(): jnp.sum(jnp.where(hits, local_of(all_pivots)[:, :, None], 0), axis=1)  5.74 us
    another operation x5, other arithmetic  4.98 us
  transfers between devices with their start and end apart: 1, of which 1 were waited for; matrix products, arithmetic and copies ran while one was open for 9% of the time, Pallas kernels for 0%

profile of v4, /device:TPU:0, one launch (start us, length us, event | category | flops | bytes accessed | tf_op | source)
XLA Modules:
  0.0 238.9 jit_solution(14687091776530043751)
XLA Ops:
  6.5 2.2 slice-done
  8.7 3.4 %copy.16 = bf16[128,8,2,1024]{3,1,2,0:T(8,128)(2,1)} copy(bf16[128,8,2,1024]{3,2,1,0:T(2,128)(2,1)S(1)} %bitcast.59) | data formatting | bytes 8388608
  12.2 3.4 %copy.17 = bf16[128,8,2,1024]{3,1,2,0:T(8,128)(2,1)} copy(bf16[128,8,2,1024]{3,2,1,0:T(2,128)(2,1)S(1)} %bitcast.61) | data formatting | bytes 8388608
  15.6 3.2 %fusion = bf16[128,2,1024]{2,1,0:T(2,128)(2,1)S(1)} fusion(f32[128,4,1,1024]{3,2,1,0:T(1,128)S(1)} %copy-done.1), kind=kLoop, calls=%fused_computation.3 | loop fusion | bytes 1048576 | tf_op jit(solution)/shard_map/slice | solution.py:364
  18.8 0.9 copy.15
  19.8 71.9 %upper.1 = (bf16[1024,2048]{1,0:T(8,128)(2,1)}, bf16[1024,1024]{1,0:T(8,128)(2,1)}) custom-call(bf16[128,2048]{1,0:T(8,128)(2,1)} %bitcast.64, bf16[1024,2048]{1,0:T(8,128)(2,1)} %bitcast.57, bf16[1024,2048]{1,0:T(8,128)(2,1)} %bitcast.58), custom_call_target="tpu_custom_call" | custom-call | tf_op jit(solution)/shard_map/upper/pallas_call | solution.py:388
  91.6 0.0 copy-start.2
  91.6 0.0 reduce-scatter.2.cloned.1.call-update
  91.7 0.7 copy-done.2
  92.3 14.5 %all-gather = s32[8,1,2048]{2,1,0:T(1,128)S(1)} all-gather(s32[1,1,2048]{2,1,0:T(1,128)S(1)} %bitcast.66), channel_id=1, replica_groups=mesh['prow'=8,'pcol'=4] {'prow'}, dimensions={0}, use_global_device_ids=true | all-gather | bytes 73728 | tf_op jit(solution)/shard_map/all_gather | solution.py:369
  106.8 0.1 convert_bitcast_fusion
  106.9 2.3 reduce-window.14
  109.2 0.3 slice_reduce_fusion.2
  109.5 0.2 reduce-window.15
  109.6 0.1 add_bitcast_fusion
  109.7 0.1 fusion.5
  109.8 5.7 %select_reduce_fusion = s32[8,256]{1,0:T(8,128)S(1)} fusion(s32[8,2048]{1,0:T(8,128)S(1)} %get-tuple-element.13, s32[8,2048]{1,0:T(8,128)S(1)} %get-tuple-element.14), kind=kLoop, calls=%fused_computation | loop fusion | flops 12580864 | bytes 139264 | tf_op jit(solution)/shard_map/reduce_sum | solution.py:380
  115.6 0.6 reshape.231.picked_ref
  116.2 2.3 reduce-window.16
  118.5 0.3 slice_reduce_fusion.1
  118.8 0.2 reduce-window.19
  118.9 2.2 slice-done.1
  121.2 3.4 %copy.18 = bf16[128,8,2,1024]{3,1,2,0:T(8,128)(2,1)} copy(bf16[128,8,2,1024]{3,2,1,0:T(2,128)(2,1)S(1)} %bitcast.60) | data formatting | bytes 8388608
  124.6 3.2 %slice_reduce_fusion = f32[128,2,1024]{2,1,0:T(2,128)S(1)} fusion(f32[128,4,1,1024]{3,2,1,0:T(1,128)S(1)} %copy-done.1), kind=kLoop, calls=%fused_computation.5 | loop fusion | bytes 2097152 | tf_op jit(solution)/shard_map/slice | solution.py:363
  127.8 0.3 copy.14
  128.1 0.1 select_reduce_fusion.1
  128.2 1.9 constant_dynamic-slice_fusion.upper_ref
  130.2 0.7 fusion.17.code_ref
  130.9 10.9 %reduce-scatter.2.cloned.1.call-done = bf16[128,2048]{1,0:T(8,128)(2,1)} async-done(((bf16[1024,2048]{1,0:T(8,128)(2,1)}), bf16[128,2048]{1,0:T(8,128)(2,1)}) %reduce-scatter.2.cloned.1.call-update) | async-done | bytes 524304 | tf_op jit(solution)/shard_map/reduce_scatter | solution.py:411
  141.7 1.9 subtract_convert_fusion.rhs_ref
  143.7 85.7 %lower.1 = bf16[256,2048]{1,0:T(8,128)(2,1)} custom-call(bf16[128,2048]{1,0:T(8,128)(2,1)} %subtract_convert_fusion.rhs_ref, bf16[1024,2048]{1,0:T(8,128)(2,1)} %bitcast.56, bf16[256,1024]{1,0:T(8,128)(2,1)} %constant_dynamic-slice_fusion.upper_ref, s32[8,1,256]{2,1,0:T(1,128)} %reshape.231.picked_ref, s32[1,2048]{1,0:T(1,128)} %fusion.17.code_ref), custom_call_target="tpu_custom_call" | custom-call | tf_op jit(solution)/shard_map/lower/pallas_call | solution.py:415
  229.4 2.6 %reshape.233 = bf16[256,2,1,1024]{3,1,0,2:T(2,128)(2,1)} reshape(bf16[256,2048]{1,0:T(8,128)(2,1)} %lower.1) | data formatting | bytes 2097152 | tf_op jit(solution)/shard_map/reshape | solution.py:433
  (10 shorter events, 0.1 us)
Async XLA Ops:
  6.5 135.2 %reduce-scatter.2.cloned.1.call-start = ((), (), s32[]{:S(2)}) async-start(), calls=%async_computation.1 | async-start | bytes 4718592 | tf_op jit(solution)/shard_map/reduce_scatter | solution.py:411
  6.5 2.2 slice-start
  8.7 3.4 %copy-start = (bf16[1,1,1024,2,1,1024]{5,3,4,2,1,0:T(2,128)(2,1)S(1)}, bf16[1,1,1024,2,1,1024]{5,3,4,2,1,0:T(2,128)(2,1)}, u32[]{:S(2)}) copy-start(bf16[1,1,1024,2,1,1024]{5,3,4,2,1,0:T(2,128)(2,1)} %param.6) | copy-start | bytes 12582916
  12.2 3.4 %copy-start.1 = (f32[128,4,1,1024]{3,2,1,0:T(1,128)S(1)}, f32[128,4,1,1024]{3,2,1,0:T(1,128)}, u32[]{:S(2)}) copy-start(f32[128,4,1,1024]{3,2,1,0:T(1,128)} %param.4) | copy-start | bytes 6291460
  91.6 0.7 copy-start.2
  118.9 2.2 slice-start.1
Sparse Core Ops, SparseCore 0:
  91.8 49.9 reduce-scatter.1
